TPU v7x, 32 devices: a whole 2x2x4 slice. The times are simulated.
32 devices in a mesh: band: 4 (over x, core), grid: 8 (over z, y).
Axes of the slice: x: 2, y: 2, z: 4, core: 2. Of those that a mesh axis runs over, the one named last changes fastest.
Arguments:
- orbitals: bfloat16 [16384, 2048], P('grid', 'band'), may hold values from -6 to 6
- projectors: bfloat16 [64, 8, 128], replicated, may hold values from -0.5 to 0.5
- sphere_start: int32 [64], replicated, may hold values from 0 to 1920, as said below
- proj_count: int32 [64], replicated, may hold values from 1 to 8
- owner_slab: int32 [64], replicated, may hold values from 0 to 7, as said below
- correlation_coef: float32 [64, 8, 8], replicated, as said below
Outputs:
- rotated: bfloat16 [16384, 2048], P(('grid', 'band'))
Inputs may be any that keep to these rules, and one draw needn't show every extreme that they name: `sphere_start`: a multiple of 128. `owner_slab`: every slab owns exactly 8 atoms. `correlation_coef`: each atom's matrix is symmetric positive definite.
All inputs are finite; a program needn't handle non-finite values.
Results may differ from a plain program's by a relative error of at most 0.0049.
Values may be sent and summed in bfloat16 or wider, within the bound.
A program may use at most 128 MiB of HBM per device.

v0:
```python
import jax
import jax.numpy as jnp
from jax import lax
from jax.sharding import PartitionSpec as P

SPH = 128
NPMAX = 8
A_SLAB = 8


def inverse_factor(matrix):
    order = matrix.shape[0]
    if order <= 512 or order % 2 != 0:
        lower = jnp.linalg.cholesky(matrix)
        identity = jnp.eye(order, dtype=matrix.dtype)
        return lax.linalg.triangular_solve(lower, identity, left_side=True, lower=True)
    half = order // 2
    upper_inv = inverse_factor(matrix[:half, :half])
    below = jnp.dot(matrix[half:, :half], upper_inv.T, precision=lax.Precision.HIGHEST)
    schur = matrix[half:, half:] - jnp.dot(below, below.T, precision=lax.Precision.HIGHEST)
    lower_inv = inverse_factor(schur)
    corner = -jnp.dot(
        lower_inv,
        jnp.dot(below, upper_inv, precision=lax.Precision.HIGHEST),
        precision=lax.Precision.HIGHEST,
    )
    top = jnp.concatenate([upper_inv, jnp.zeros((half, order - half), matrix.dtype)], axis=1)
    bottom = jnp.concatenate([corner, lower_inv], axis=1)
    return jnp.concatenate([top, bottom], axis=0)


def slab_atoms(owner_slab, slab):
    atoms = owner_slab.shape[0]
    keyed = jnp.where(owner_slab == slab, 0, 1) * atoms + jnp.arange(atoms, dtype=jnp.int32)
    return jnp.argsort(keyed, stable=True)[:A_SLAB]


def atom_terms(source, weights, starts, counts, coefs, valid):

    def take_rows(offset):
        return lax.dynamic_slice_in_dim(source, offset, SPH, 0)

    sphere_rows = jax.vmap(take_rows)(starts)
    correlations = jnp.einsum(
        "aij,ajn->ain", weights, sphere_rows, preferred_element_type=jnp.float32
    )
    active = (jnp.arange(NPMAX)[None, :] < counts[:, None]) & valid[:, None]
    correlations = jnp.where(active[:, :, None], correlations, jnp.zeros_like(correlations))
    weighted = jnp.einsum("aij,ajn->ain", coefs, correlations, precision=lax.Precision.HIGHEST)
    return (correlations, weighted)


def shards(orbitals, projectors, sphere_start, proj_count, owner_slab, correlation_coef):
    band_index = lax.axis_index("band")
    slab = lax.axis_index("grid")
    total_rows = orbitals.shape[0] * lax.axis_size("grid")
    chosen = slab_atoms(owner_slab, slab)
    weights = projectors[chosen]
    counts = proj_count[chosen]
    coefs = correlation_coef[chosen]
    mine = lax.all_to_all(orbitals, "band", split_axis=0, concat_axis=1, tiled=True)
    height = mine.shape[0]
    width_all = mine.shape[1]
    gram = jnp.dot(mine.T, mine, preferred_element_type=jnp.float32) * (1.0 / total_rows)
    offsets = sphere_start[chosen] - band_index * height
    valid = (offsets >= 0) & (offsets < height)
    offsets = jnp.clip(offsets, 0, height - SPH)
    correlations, weighted = atom_terms(mine, weights, offsets, counts, coefs, valid)
    paw = jnp.dot(
        weighted.reshape(-1, width_all).T,
        correlations.reshape(-1, width_all),
        precision=lax.Precision.HIGHEST,
    )
    metric = lax.psum(gram + paw, ("band", "grid"))
    inverse = inverse_factor(metric).astype(jnp.bfloat16)
    return jnp.dot(mine, inverse.T, preferred_element_type=jnp.float32).astype(jnp.bfloat16)


def solution(mesh):
    in_specs = (P("grid", "band"), P(), P(), P(), P(), P())
    out_specs = P(("grid", "band"), None)
    return jax.shard_map(shards, mesh=mesh, in_specs=in_specs, out_specs=out_specs, check_vma=False)
```

profile of v0, /device:TPU:0, one launch (start us, length us, event | category | flops | bytes accessed | tf_op | source)
XLA Modules:
  0.0 1109.8 jit_solution(1387231611529632680)
XLA Ops:
  16.0 21.5 %all-to-all-done = bf16[4,512,512]{2,1,0:T(8,128)(2,1)} async-done(((bf16[4,512,512]{2,1,0:T(8,128)(2,1)}), bf16[4,512,512]{2,1,0:T(8,128)(2,1)}, u32[]{:S(2)}, u32[]{:S(2)}) %all-to-all-start) | async-done | bytes 2097184 | tf_op jit(solution)/shard_map/all_to_all | solution.py:61
  40.3 20.2 %while.9 = (s32[]{:T(128)}, bf16[512,2048]{0,1:T(8,128)(2,1)S(1)}, s32[8,2]{0,1:T(2,128)S(1)}, bf16[8,128,2048]{2,1,0:T(8,128)(2,1)}, s32[]{:T(128)}) while((s32[]{:T(128)}, bf16[512,2048]{0,1:T(8,128)(2,1)S(1)}, s32[8,2]{0,1:T(2,128)S(1)}, bf16[8,128,2048]{2,1,0:T(8,128)(2,1)}, s32[]{:T(128)}) %tuple.122), condition=%wide.while_cond.1, body=%wide.while_body.1.sunk | while | flops 2 | bytes 3146333 | solution.py:41
  64.7 14.1 %fusion.178 = f32[2048,2048,1]{0,1,2:T(8,128)S(1)} fusion(f32[8,8,2048]{2,1,0:T(8,128)S(1)} %fusion.177, f32[8,8,2048]{2,1,0:T(8,128)S(1)} %convolution_select_fusion), kind=kOutput, calls=%fused_computation.329 | convolution fusion | flops 3221225472 | bytes 17825792 | tf_op jit(solution)/shard_map/dot_general | solution.py:69
  78.8 12.9 %bitcast_add_fusion = f32[2048,2048]{0,1:T(8,128)} fusion(f32[2048,2048,1]{0,1,2:T(8,128)S(1)} %fusion.178, bf16[512,2048]{0,1:T(8,128)(2,1)} %copy-done.4), kind=kOutput, calls=%fused_computation.16 | convolution fusion | flops 4303355904 | bytes 35651584 | tf_op jit(solution)/shard_map/dot_general | solution.py:64
  91.9 279.4 %all-reduce.7.cloned.1.call-done = f32[2048,2048]{0,1:T(8,128)} async-done(((f32[2048,2048]{0,1:T(8,128)}), f32[2048,2048]{0,1:T(8,128)}) %all-reduce.7.cloned.1.call-update) | async-done | bytes 16777232 | tf_op jit(solution)/shard_map/psum | solution.py:74
  374.4 11.7 %cholesky.462 = f32[128,128]{1,0:T(8,128)S(1)} custom-call(f32[128,128]{1,0:T(8,128)S(1)} %cholesky.746), custom_call_target="Cholesky" | custom-call | tf_op jit(solution)/shard_map/jit(cholesky)/cholesky | solution.py:14
  396.9 11.7 %cholesky.481 = f32[128,128]{1,0:T(8,128)S(1)} custom-call(f32[128,128]{1,0:T(8,128)S(1)} %cholesky.750), custom_call_target="Cholesky" | custom-call | tf_op jit(solution)/shard_map/jit(cholesky)/cholesky | solution.py:14
  419.1 11.9 %cholesky.502 = f32[128,128]{1,0:T(8,128)S(1)} custom-call(f32[128,128]{1,0:T(8,128)S(1)} %cholesky.755), custom_call_target="Cholesky" | custom-call | tf_op jit(solution)/shard_map/jit(cholesky)/cholesky | solution.py:14
  442.1 11.7 %cholesky.519 = f32[128,128]{1,0:T(8,128)S(1)} custom-call(f32[128,128]{1,0:T(8,128)S(1)} %convolution_subtract_fusion.25), custom_call_target="Cholesky" | custom-call | tf_op jit(solution)/shard_map/jit(cholesky)/cholesky | solution.py:14
  466.0 39.7 %custom-call.38 = f32[4,128,128]{1,2,0:T(8,128)S(1)} custom-call(f32[4,128,128]{2,1,0:T(8,128)S(1)} %get-tuple-element.43), custom_call_target="InvertDiagBlocksLowerTriangular" | custom-call | tf_op jit(solution)/shard_map/triangular_solve/custom-call.3 | solution.py:16
  523.4 11.9 %cholesky.534 = f32[128,128]{1,0:T(8,128)S(1)} custom-call(f32[128,128]{1,0:T(8,128)S(1)} %cholesky.759), custom_call_target="Cholesky" | custom-call | tf_op jit(solution)/shard_map/jit(cholesky)/cholesky | solution.py:14
  547.8 11.7 %cholesky.553 = f32[128,128]{1,0:T(8,128)S(1)} custom-call(f32[128,128]{1,0:T(8,128)S(1)} %cholesky.763), custom_call_target="Cholesky" | custom-call | tf_op jit(solution)/shard_map/jit(cholesky)/cholesky | solution.py:14
  572.3 12.1 %cholesky.574 = f32[128,128]{1,0:T(8,128)S(1)} custom-call(f32[128,128]{1,0:T(8,128)S(1)} %cholesky.768), custom_call_target="Cholesky" | custom-call | tf_op jit(solution)/shard_map/jit(cholesky)/cholesky | solution.py:14
  596.4 11.7 %cholesky.591 = f32[128,128]{1,0:T(8,128)S(1)} custom-call(f32[128,128]{1,0:T(8,128)S(1)} %convolution_subtract_fusion.24), custom_call_target="Cholesky" | custom-call | tf_op jit(solution)/shard_map/jit(cholesky)/cholesky | solution.py:14
  624.0 39.3 %custom-call.42 = f32[4,128,128]{1,2,0:T(8,128)S(1)} custom-call(f32[4,128,128]{2,1,0:T(8,128)S(1)} %get-tuple-element.44), custom_call_target="InvertDiagBlocksLowerTriangular" | custom-call | tf_op jit(solution)/shard_map/triangular_solve/custom-call.3 | solution.py:16
  672.0 28.8 %fusion.9 = f32[1024,1024]{1,0:T(8,128)S(1)} fusion(f32[2048,2048]{0,1:T(8,128)} %all-reduce.7.cloned.1.call-done, f32[512,512]{1,0:T(8,128)S(1)} %copy-done.9, f32[128,512]{1,0:T(8,128)S(1)} %fusion.126, f32[128,512]{1,0:T(8,128)S(1)} %fusion.127, f32[128,512]{1,0:T(8,128)S(1)} %fusion.129, f32[128,512]{1,0:T(8,128)S(1)} %fusion.82, ...), kind=kOutput, calls=%fused_computation.26 | convolution fusion | flops 12892241920 | bytes 11534336 | tf_op jit(solution)/shard_map/dot_general | solution.py:19
  700.9 16.8 %fusion.171 = f32[1024,1024]{1,0:T(8,128)} fusion(f32[1024,1024]{1,0:T(8,128)S(1)} %fusion.9, f32[512,512]{1,0:T(8,128)S(1)} %copy-done.9, f32[128,512]{1,0:T(8,128)S(1)} %fusion.126, f32[128,512]{1,0:T(8,128)S(1)} %fusion.127, f32[128,512]{1,0:T(8,128)S(1)} %fusion.129, f32[128,512]{1,0:T(8,128)S(1)} %fusion.82, f32[512,512]{1,0:T(8,128)S(1)} %convolution_negate_fusion.1), kind=kOutput, calls=%fused_computation.322 | convolution fusion | flops 12892241920 | bytes 11534336 | tf_op jit(solution)/shard_map/dot_general | solution.py:24
  717.7 15.8 %slice_subtract_fusion = f32[1024,1024]{0,1:T(8,128)S(1)} fusion(f32[2048,2048]{0,1:T(8,128)} %all-reduce.7.cloned.1.call-done, f32[1024,1024]{1,0:T(8,128)S(1)} %fusion.9), kind=kOutput, calls=%fused_computation.28 | convolution fusion | flops 12885950464 | bytes 16777216 | tf_op jit(solution)/shard_map/dot_general | solution.py:20
  740.4 11.7 %cholesky.606 = f32[128,128]{1,0:T(8,128)S(1)} custom-call(f32[128,128]{1,0:T(8,128)S(1)} %cholesky.772), custom_call_target="Cholesky" | custom-call | tf_op jit(solution)/shard_map/jit(cholesky)/cholesky | solution.py:14
  764.7 11.7 %cholesky.625 = f32[128,128]{1,0:T(8,128)S(1)} custom-call(f32[128,128]{1,0:T(8,128)S(1)} %cholesky.776), custom_call_target="Cholesky" | custom-call | tf_op jit(solution)/shard_map/jit(cholesky)/cholesky | solution.py:14
  841.0 39.3 %custom-call.46 = f32[4,128,128]{1,2,0:T(8,128)S(1)} custom-call(f32[4,128,128]{2,1,0:T(8,128)S(1)} %get-tuple-element.45), custom_call_target="InvertDiagBlocksLowerTriangular" | custom-call | tf_op jit(solution)/shard_map/triangular_solve/custom-call.3 | solution.py:16
  1007.5 39.3 %custom-call.50 = f32[4,128,128]{1,2,0:T(8,128)S(1)} custom-call(f32[4,128,128]{2,1,0:T(8,128)S(1)} %get-tuple-element.46), custom_call_target="InvertDiagBlocksLowerTriangular" | custom-call | tf_op jit(solution)/shard_map/triangular_solve/custom-call.3 | solution.py:16
  1060.6 13.6 %negate_convert_fusion = bf16[1024,1024]{1,0:T(8,128)(2,1)S(1)} fusion(f32[1024,1024]{1,0:T(8,128)S(1)} %copy-done.23, f32[512,512]{1,0:T(8,128)S(1)} %copy-done.11, f32[128,512]{1,0:T(8,128)S(1)} %fusion.114, f32[128,512]{1,0:T(8,128)S(1)} %fusion.115, f32[128,512]{1,0:T(8,128)S(1)} %fusion.117, f32[128,512]{1,0:T(8,128)S(1)} %fusion.78, ...), kind=kOutput, calls=%fused_computation.32 | convolution fusion | flops 12894339072 | bytes 9437184 | tf_op jit(solution)/shard_map/dot_general | solution.py:22
  1074.3 25.8 %fusion.15 = bf16[512,2048]{0,1:T(8,128)(2,1)S(1)} fusion(bf16[512,2048]{0,1:T(8,128)(2,1)S(1)} %copy-done.5, bf16[1024,1024]{1,0:T(8,128)(2,1)S(1)} %copy-done.19, bf16[1024,1024]{1,0:T(8,128)(2,1)S(1)} %fusion.18, bf16[1024,1024]{1,0:T(8,128)(2,1)S(1)} %negate_convert_fusion), kind=kOutput, calls=%fused_computation.34 | convolution fusion | flops 4329570304 | bytes 10485760 | tf_op jit(solution)/shard_map/dot_general | solution.py:76
  (312 shorter events, 423.1 us)
Async XLA Ops:
  6.5 8.1 copy-start
  6.5 4.7 copy-start.22
  6.5 6.8 copy-start.2
  6.5 7.4 copy-start.3
  6.5 8.7 copy-start.21
  6.5 31.0 %all-to-all-start = ((bf16[4,512,512]{2,1,0:T(8,128)(2,1)}), bf16[4,512,512]{2,1,0:T(8,128)(2,1)}, u32[]{:S(2)}, u32[]{:S(2)}) async-start(bf16[4,512,512]{2,1,0:T(8,128)(2,1)} %bitcast.231), calls=%async_computation | async-start | bytes 4194304 | tf_op jit(solution)/shard_map/all_to_all | solution.py:61
  11.1 360.1 %all-reduce.7.cloned.1.call-start = ((), (), s32[]{:S(2)}) async-start(), calls=%async_computation.1 | async-start | bytes 33554432 | tf_op jit(solution)/shard_map/psum | solution.py:74
  60.5 3.6 copy-start.4
  522.4 1.0 copy-start.14
  663.4 3.5 copy-start.20
  663.8 8.2 copy-start.9
  670.1 30.7 %copy-start.17 = (f32[128,512]{1,0:T(8,128)}, f32[128,512]{1,0:T(8,128)S(1)}, u32[]{:S(2)}) copy-start(f32[128,512]{1,0:T(8,128)S(1)} %fusion.126) | copy-start | bytes 786436
  672.0 28.9 %copy-start.6 = (f32[512,512]{1,0:T(8,128)}, f32[512,512]{1,0:T(8,128)S(1)}, u32[]{:S(2)}) copy-start(f32[512,512]{1,0:T(8,128)S(1)} %convolution_negate_fusion.1) | copy-start | bytes 3145732
  733.5 1.9 copy-start.12
  880.3 7.1 copy-start.13
  891.0 4.8 copy-start.7
  891.0 4.8 copy-start.10
  891.0 4.8 copy-start.18
  994.4 58.3 %copy-start.8 = (f32[512,512]{1,0:T(8,128)S(1)}, f32[512,512]{1,0:T(8,128)}, u32[]{:S(2)}) copy-start(f32[512,512]{1,0:T(8,128)} %fusion.169) | copy-start | bytes 3145732
  1047.2 7.4 copy-start.11
  1052.7 7.9 copy-start.23
  1060.6 13.7 %copy-start.5 = (bf16[512,2048]{0,1:T(8,128)(2,1)S(1)}, bf16[512,2048]{0,1:T(8,128)(2,1)}, u32[]{:S(2)}) copy-start(bf16[512,2048]{0,1:T(8,128)(2,1)} %copy-done.4) | copy-start | bytes 6291460
  1060.6 13.7 %copy-start.19 = (bf16[1024,1024]{1,0:T(8,128)(2,1)S(1)}, bf16[1024,1024]{1,0:T(8,128)(2,1)}, u32[]{:S(2)}) copy-start(bf16[1024,1024]{1,0:T(8,128)(2,1)} %fusion.172) | copy-start | bytes 6291460
  1074.3 28.2 %copy-start.1 = (bf16[64,8,128]{2,1,0:T(8,128)(2,1)S(1)}, bf16[64,8,128]{2,1,0:T(8,128)(2,1)}, u32[]{:S(2)}) copy-start(bf16[64,8,128]{2,1,0:T(8,128)(2,1)} %param.10) | copy-start | bytes 393220
  (2 other events, 2.0 us)
Sparse Core Ops, SparseCore 0:
  91.8 279.3 all-reduce.6
where the time goes:
time: 1120 us; the launch traced here: 1110 us
  other arithmetic  502 us (45%)
  waiting for transfers between devices  301 us (27%)
  matrix products  194 us (17%)
  local copies, waits for them, and re-layouts  83.1 us (7%)
  between operations  25.2 us (2%)
    another operation x59, other arithmetic, inverse_factor(): lower = jnp.linalg.cholesky(matrix)  317 us
    psum x1, waiting for transfers between devices, shards(): metric = lax.psum(gram + paw, ('band', 'grid'))  279 us
    another operation x11, other arithmetic, inverse_factor(): lax.linalg.triangular_solve(lower, identity, left_side=True, lower=True)  163 us
    another operation x53, local copies, waits for them, and re-layouts, inverse_factor(): lax.linalg.triangular_solve(lower, identity, left_side=True, lower=True)  42.9 us
    dot_general x3, matrix products, inverse_factor(): jnp.dot(matrix[half:, :half], upper_inv.T, precision=lax.Precision.HIGHEST)  37.1 us
    dot_general x1, matrix products, shards(): jnp.dot(mine, inverse.T, preferred_element_type=jnp.float32)  25.8 us
  transfers between devices with their start and end apart: 2, of which 2 were waited for; matrix products, arithmetic and copies ran while one was open for 0% of the time, Pallas kernels for 0%

commit v1 on v0

v1 whole, which is shorter than its diff:
```python
import jax
import jax.numpy as jnp
from jax import lax
from jax.experimental import pallas as pl
from jax.experimental.pallas import tpu as pltpu
from jax.sharding import PartitionSpec as P

SPH = 128
NPMAX = 8
A_SLAB = 8
BLK = 256
TOL = 4e-6
STEPS = 10


def bdot(a, b, dims):
    return lax.dot_general(
        a.astype(jnp.bfloat16), b.astype(jnp.bfloat16), (dims, ((), ())),
        preferred_element_type=jnp.float32,
    )


def split_bf16(a):
    high = a.astype(jnp.bfloat16)
    return high, (a - high.astype(jnp.float32)).astype(jnp.bfloat16)


def bdot3(a, b, dims):
    ah, al = split_bf16(a)
    bh, bl = split_bf16(b)
    return bdot(ah, bh, dims) + (bdot(ah, bl, dims) + bdot(al, bh, dims))


def block_inverse(a, w_ref):
    rows = lax.broadcasted_iota(jnp.int32, a.shape, 0)
    cols = lax.broadcasted_iota(jnp.int32, a.shape, 1)
    diag = rows == cols
    phi_mask = jnp.where(rows > cols, 1.0, jnp.where(diag, 0.5, 0.0))
    on_diag = jnp.where(diag, a, 0.0)
    scale_col = lax.rsqrt(jnp.sum(on_diag, axis=1, keepdims=True))
    scale_row = lax.rsqrt(jnp.sum(on_diag, axis=0, keepdims=True))
    e0 = jnp.where(diag, 0.0, a * scale_col * scale_row)

    def residual(v, dot=bdot):
        t = dot(v, e0, ((1,), (0,)))
        return (
            e0 + v + jnp.where(diag, v, 0.0) + t + dot(e0 + v + t, v, ((1,), (1,)))
        ) * phi_mask

    def step(carry):
        v, phi, _, count = carry
        v = v - phi - bdot(phi, v, ((1,), (0,)))
        phi = residual(v)
        return v, phi, jnp.sum(phi * phi), count + 1

    v = -e0 * phi_mask
    phi = residual(v)
    start = (v, phi, jnp.sum(phi * phi), jnp.int32(0))
    v, phi, err, _ = lax.while_loop(
        lambda c: jnp.logical_and(jnp.logical_not(c[2] < TOL), c[3] < STEPS), step, start
    )
    v = v - phi
    phi = residual(v, bdot3)
    v = v - phi - bdot(phi, v, ((1,), (0,)))
    w_ref[...] = (v + jnp.where(diag, 1.0, 0.0)) * scale_row

    @pl.when(jnp.logical_not(err < TOL))
    def _():
        w_ref[...] = jnp.where(rows <= cols, a, 0.0)

        def column(j, _):
            b = w_ref[...]
            line = jnp.sum(jnp.where(rows == j, b, 0.0), axis=0, keepdims=True)
            lane = lax.broadcasted_iota(jnp.int32, line.shape, 1)
            pivot = jnp.sum(jnp.where(lane == j, line, 0.0), axis=1, keepdims=True)
            q = jnp.where(lane == j, 1.0, line) * lax.rsqrt(pivot)
            spread = jnp.broadcast_to(q, b.shape)
            factor = jnp.sum(jnp.where(diag, spread, 0.0), axis=1, keepdims=True)
            keep = (cols <= j) | (cols >= rows)
            below = b - jnp.where(keep, factor * q, 0.0)
            w_ref[...] = jnp.where(rows == j, q, jnp.where(rows > j, below, b))
            return 0

        lax.fori_loop(0, a.shape[0], column, 0)
        w_ref[...] = jnp.where(rows >= cols, w_ref[...], 0.0)


def factor_kernel(packed_ref, out_ref, work, wblk, q):
    n = out_ref.shape[0]
    blocks = n // BLK
    for i in range(blocks // 2):
        band = slice(i * BLK, (i + 1) * BLK)
        j = blocks - 1 - i
        cut = n - i * BLK
        for row, lo, hi in ((i, 0, cut), (j, cut, n + BLK)):
            rows = slice(row * BLK, (row + 1) * BLK)
            if row:
                work[rows, : row * BLK] = jnp.zeros((BLK, row * BLK), jnp.float32)
            work[rows, row * BLK :] = packed_ref[band, lo:hi].astype(jnp.float32)

    def at(i):
        return pl.ds(pl.multiple_of(i * BLK, BLK), BLK)

    def pivot(k, _):
        block_inverse(work[at(k), at(k)], wblk)
        w = wblk[...]

        def line(j, _):
            q[:, at(j)] = bdot3(w, work[at(k), at(j)], ((1,), (0,))).astype(jnp.bfloat16)
            return 0

        lax.fori_loop(0, blocks, line, 0)
        q[:, at(k)] = w.astype(jnp.bfloat16)

        def store(j, _):
            out_ref[at(k), at(j)] = q[:, at(j)]
            return 0

        def clear(j, _):
            out_ref[at(k), at(j)] = jnp.zeros((BLK, BLK), jnp.bfloat16)
            return 0

        lax.fori_loop(0, k + 1, store, 0)
        lax.fori_loop(k + 1, blocks, clear, 0)

        def below(i, _):
            p = q[:, at(i)].T

            def update(j, _):
                work[at(i), at(j)] -= bdot(p, q[:, at(j)], ((1,), (0,)))
                return 0

            lax.fori_loop(0, k + 1, update, 0)
            lax.fori_loop(i, blocks, update, 0)
            return 0

        lax.fori_loop(k + 1, blocks, below, 0)
        return 0

    lax.fori_loop(0, blocks, pivot, 0)


def inverse_of_packed(packed, n):
    return pl.pallas_call(
        factor_kernel,
        out_shape=jax.ShapeDtypeStruct((n, n), jnp.bfloat16),
        in_specs=[pl.BlockSpec(memory_space=pltpu.VMEM)],
        out_specs=pl.BlockSpec(memory_space=pltpu.VMEM),
        scratch_shapes=[
            pltpu.VMEM((n, n), jnp.float32),
            pltpu.VMEM((BLK, BLK), jnp.float32),
            pltpu.VMEM((BLK, n), jnp.bfloat16),
        ],
        compiler_params=pltpu.CompilerParams(vmem_limit_bytes=56 * 1024 * 1024),
        name="inverse_factor",
    )(packed)


def slab_atoms(owner_slab, slab):
    mine = owner_slab == slab
    place = jnp.cumsum(mine.astype(jnp.int32)) - 1
    atoms = jnp.arange(owner_slab.shape[0], dtype=jnp.int32)
    hit = mine[None, :] & (place[None, :] == jnp.arange(A_SLAB, dtype=jnp.int32)[:, None])
    return jnp.sum(jnp.where(hit, atoms[None, :], 0), axis=1)


def atom_terms(source, weights, starts, counts, coefs):
    height = source.shape[0]
    atoms = weights.shape[0]
    active = jnp.arange(NPMAX)[None, :] < counts[:, None]
    here = jnp.arange(height // SPH)[None, :] * SPH == starts[:, None]
    keep = active[:, :, None, None] & here[:, None, :, None]
    spread = jnp.where(keep, weights[:, :, None, :], jnp.zeros((), weights.dtype))
    correlations = jnp.dot(
        spread.reshape(atoms * NPMAX, height), source, preferred_element_type=jnp.float32
    )
    same = jnp.eye(atoms, dtype=coefs.dtype)
    mixing = (same[:, None, :, None] * coefs[:, :, None, :]).reshape(atoms * NPMAX, -1)
    weighted = jnp.dot(mixing, correlations, precision=lax.Precision.HIGHEST)
    return (correlations, weighted)


def split_terms(x):
    high = lax.reduce_precision(x, 8, 7)
    return high.astype(jnp.bfloat16), (x - high).astype(jnp.bfloat16)


def shards(orbitals, projectors, sphere_start, proj_count, owner_slab, correlation_coef):
    band_index = lax.axis_index("band")
    slab = lax.axis_index("grid")
    total_rows = orbitals.shape[0] * lax.axis_size("grid")
    chosen = slab_atoms(owner_slab, slab)
    weights = projectors[chosen]
    counts = proj_count[chosen]
    coefs = correlation_coef[chosen]
    mine = lax.all_to_all(orbitals, "band", split_axis=0, concat_axis=1, tiled=True)
    height, width_all = mine.shape
    offsets = sphere_start[chosen] - band_index * height
    correlations, weighted = atom_terms(mine, weights, offsets, counts, coefs)
    wh, wl = split_terms(weighted * total_rows)
    ch, cl = split_terms(correlations)
    left = jnp.concatenate([mine, wh, wh, wl], axis=0)
    right = jnp.concatenate([mine, ch, cl, ch], axis=0)
    blocks = width_all // BLK

    def strip(i):
        rows = left[:, i * BLK : (i + 1) * BLK]
        return lax.dot_general(
            rows, right[:, i * BLK :], (((0,), (0,)), ((), ())),
            preferred_element_type=jnp.float32,
        ) * (1.0 / total_rows)

    packed = jnp.concatenate(
        [
            jnp.concatenate([strip(i), strip(blocks - 1 - i)], axis=1)
            for i in range(blocks // 2)
        ],
        axis=0,
    )
    part = lax.psum_scatter(packed, ("grid", "band"), scatter_dimension=0, tiled=True)
    whole = lax.all_gather(part, ("grid", "band"), axis=0, tiled=True)
    inverse = inverse_of_packed(whole, width_all)
    return lax.dot_general(
        mine, inverse, (((1,), (1,)), ((), ())), preferred_element_type=jnp.float32
    ).astype(jnp.bfloat16)


def solution(mesh):
    in_specs = (P("grid", "band"), P(), P(), P(), P(), P())
    out_specs = P(("grid", "band"), None)
    return jax.shard_map(shards, mesh=mesh, in_specs=in_specs, out_specs=out_specs, check_vma=False)
```

time: 1120 us -> 467 us (0.42)
  other arithmetic: 502 us -> 11.5 us
  matrix products: 194 us -> 18.2 us
  Pallas kernels: 0 us -> 159 us
  local copies, waits for them, and re-layouts: 83.1 us -> 16.8 us
  waiting for transfers between devices: 301 us -> 242 us
  between operations: 25.2 us -> 13.6 us
    another operation x72 -> x2, other arithmetic: 494 us -> 0.1 us  [the longest x59 317 us: inverse_factor(): lower = jnp.linalg.cholesky(matrix)]
    psum x1 -> x0, waiting for transfers between devices: 279 us -> none  [shards(): metric = lax.psum(gram + paw, ('band', 'grid'))]
    pallas_call x0 -> x1, Pallas kernels: none -> 159 us  [inverse_of_packed(): pl.pallas_call(factor_kernel, out_shape=jax.ShapeDtypeStruct((n, n), jnp....]
    reduce_scatter x0 -> x1, waiting for transfers between devices: none -> 137 us  [shards(): lax.psum_scatter(packed, ('grid', 'band'), scatter_dimension=0, tiled=True)]
    dot_general x17 -> x11, matrix products: 154 us -> 18.2 us  [the longest x1 9.1 us: shards(): lax.dot_general(mine, inverse, (((1,), (1,)), ((), ())), preferred_elemen...]
    all_gather x0 -> x1, waiting for transfers between devices: none -> 83.4 us  [shards(): whole = lax.all_gather(part, ('grid', 'band'), axis=0, tiled=True)]
    another operation x69 -> x1, local copies, waits for them, and re-layouts: 43.5 us -> 0.1 us  [the longest x53 42.9 us: inverse_factor(): lax.linalg.triangular_solve(lower, identity, left_side=True, lower=True)]
    another operation x52 -> x0, matrix products: 39.9 us -> none  [the longest x28 21.7 us: inverse_factor(): lax.linalg.triangular_solve(lower, identity, left_side=True, lower=True)]
  transfers between devices with their start and end apart: 2 -> 3, of which waited for: 2 -> 3; matrix products, arithmetic and copies ran while one was open for 0% -> 1% of each run, Pallas kernels for 0% -> 0%
where the time goes in v1:
time: 467 us; the launch traced here: 466 us
  waiting for transfers between devices  242 us (52%)
  Pallas kernels  159 us (34%)
  matrix products  18.2 us (4%)
  local copies, waits for them, and re-layouts  16.8 us (4%)
  between operations  13.6 us (3%)
  other arithmetic  11.5 us (2%)
    pallas_call x1, Pallas kernels, inverse_of_packed(): pl.pallas_call(factor_kernel, out_shape=jax.ShapeDtypeStruct((n, n), jnp....  159 us
    reduce_scatter x1, waiting for transfers between devices, shards(): lax.psum_scatter(packed, ('grid', 'band'), scatter_dimension=0, tiled=True)  137 us
    all_gather x1, waiting for transfers between devices, shards(): whole = lax.all_gather(part, ('grid', 'band'), axis=0, tiled=True)  83.4 us
    all_to_all x1, waiting for transfers between devices, shards(): lax.all_to_all(orbitals, 'band', split_axis=0, concat_axis=1, tiled=True)  21.4 us
  transfers between devices with their start and end apart: 3, of which 3 were waited for; matrix products, arithmetic and copies ran while one was open for 1% of the time, Pallas kernels for 0%

profile of v1, /device:TPU:0, one launch (start us, length us, event | category | flops | bytes accessed | tf_op | source)
XLA Modules:
  0.0 466.1 jit_solution(3281960996689098958)
XLA Ops:
  6.5 4.4 all-to-all-start
  11.4 0.6 gather_fusion.2
  12.1 0.6 gather_fusion.1
  14.1 0.7 mul.85
  15.2 21.4 %all-to-all-done = bf16[4,512,512]{2,1,0:T(8,128)(2,1)S(1)} async-done(((bf16[4,512,512]{2,1,0:T(8,128)(2,1)}), bf16[4,512,512]{2,1,0:T(8,128)(2,1)S(1)}, u32[]{:S(2)}, u32[]{:S(2)}) %all-to-all-start) | async-done | bytes 2097184 | tf_op jit(solution)/shard_map/all_to_all | solution.py:196
  36.6 1.3 copy-done.3
  37.9 2.8 copy.30
  40.7 1.5 fusion.16
  42.2 1.2 copy.37
  43.4 2.1 reduce-precision_convert_fusion.1
  45.5 2.0 copy.33
  47.8 2.0 copy.35
  49.7 3.9 fusion.1
  54.9 0.6 fusion.10
  55.6 1.0 convolution_multiply_fusion.3
  56.6 0.8 convolution_multiply_fusion
  57.4 0.8 convolution_multiply_fusion.1
  58.2 1.0 convolution_multiply_fusion.2
  59.2 6.7 %maximum_maximum_fusion = f32[1024,2304]{1,0:T(8,128)} fusion(f32[256,1024]{1,0:T(8,128)S(1)} %fusion.10, f32[256,1280]{1,0:T(8,128)S(1)} %convolution_multiply_fusion, f32[256,768]{1,0:T(8,128)S(1)} %convolution_multiply_fusion.5, f32[256,1536]{1,0:T(8,128)S(1)} %convolution_multiply_fusion.1, f32[256,512]{1,0:T(8,128)S(1)} %convolution_multiply_fusion.6, ...), kind=kLoop, calls=%fused_computation.4 | loop fusion | flops 16515072 | bytes 18874368 | tf_op jit(solution)/shard_map/concatenate | solution.py:213
  66.2 137.3 %reduce-scatter.2.cloned.1.call-done = f32[32,2304]{1,0:T(8,128)} async-done(((f32[1024,2304]{1,0:T(8,128)}), f32[32,2304]{1,0:T(8,128)}) %reduce-scatter.2.cloned.1.call-update) | async-done | bytes 294928 | tf_op jit(solution)/shard_map/reduce_scatter | solution.py:220
  203.5 83.4 %all-gather.2.cloned.1.call-done.packed_ref = f32[1024,2304]{1,0:T(8,128)} async-done(((f32[32,2304]{1,0:T(8,128)}), f32[1024,2304]{1,0:T(8,128)}) %all-gather.2.cloned.1.call-update) | async-done | bytes 9437200 | tf_op jit(solution)/shard_map/all_gather | solution.py:221
  286.9 159.4 %inverse_factor.1 = bf16[2048,2048]{1,0:T(8,128)(2,1)} custom-call(f32[1024,2304]{1,0:T(8,128)} %all-gather.2.cloned.1.call-done.packed_ref), custom_call_target="tpu_custom_call" | custom-call | tf_op jit(solution)/shard_map/inverse_factor/pallas_call | solution.py:144
  446.2 9.1 %fusion.5 = bf16[512,2048]{0,1:T(8,128)(2,1)} fusion(bf16[2048,2048]{1,0:T(8,128)(2,1)} %inverse_factor.1, bf16[512,2048]{0,1:T(8,128)(2,1)S(1)} %bitcast.29), kind=kOutput, calls=%fused_computation.16 | convolution fusion | flops 4296015872 | bytes 12582912 | tf_op jit(solution)/shard_map/dot_general | solution.py:223
  455.3 3.9 copy.40
  (37 shorter events, 4.0 us)
Async XLA Ops:
  6.5 6.2 %copy-start = (bf16[64,8,128]{2,1,0:T(8,128)(2,1)S(1)}, bf16[64,8,128]{2,1,0:T(8,128)(2,1)}, u32[]{:S(2)}) copy-start(bf16[64,8,128]{2,1,0:T(8,128)(2,1)} %param.7) | copy-start | bytes 393220
  6.5 4.4 copy-start.5
  6.5 4.9 %copy-start.1 = (s32[64]{0:T(128)S(1)}, s32[64]{0:T(128)}, u32[]{:S(2)}) copy-start(s32[64]{0:T(128)} %param.8) | copy-start | bytes 772
  6.5 5.5 %copy-start.2 = (s32[64]{0:T(128)S(1)}, s32[64]{0:T(128)}, u32[]{:S(2)}) copy-start(s32[64]{0:T(128)} %param.9) | copy-start | bytes 772
  6.5 6.7 %copy-start.4 = (f32[64,8,8]{0,2,1:T(8,128)S(1)}, f32[64,8,8]{0,2,1:T(8,128)}, u32[]{:S(2)}) copy-start(f32[64,8,8]{0,2,1:T(8,128)} %param.11) | copy-start | bytes 49156
  6.5 30.1 %all-to-all-start = ((bf16[4,512,512]{2,1,0:T(8,128)(2,1)}), bf16[4,512,512]{2,1,0:T(8,128)(2,1)S(1)}, u32[]{:S(2)}, u32[]{:S(2)}) async-start(bf16[4,512,512]{2,1,0:T(8,128)(2,1)} %bitcast.31), calls=%async_computation | async-start | bytes 4194304 | tf_op jit(solution)/shard_map/all_to_all | solution.py:196
  10.9 192.5 %reduce-scatter.2.cloned.1.call-start = ((), (), s32[]{:S(2)}) async-start(), calls=%async_computation.2 | async-start | bytes 9732096 | tf_op jit(solution)/shard_map/reduce_scatter | solution.py:220
  36.6 1.3 copy-start.3
  66.0 220.9 %all-gather.2.cloned.1.call-start = ((), (), s32[]{:S(2)}) async-start(), calls=%async_computation.3 | async-start | bytes 9732096 | tf_op jit(solution)/shard_map/all_gather | solution.py:221
Sparse Core Ops, SparseCore 0:
  66.1 137.3 reduce-scatter.1
  206.4 80.4 all-gather.1
